TPU v7x, 256 devices: a whole 4x4x8 slice. The times are simulated.
256 devices in a mesh: tok: 64 (over x, z, core), head: 4 (over y).
Axes of the slice: x: 4, y: 4, z: 8, core: 2. Of those that a mesh axis runs over, the one named last changes fastest.
Arguments:
- queries: bfloat16 [2, 8192, 2048], P(None, 'tok', 'head'), may hold values from -16 to 16
- keys: bfloat16 [8192, 2048], P('tok', 'head'), may hold values from -16 to 16
- values: bfloat16 [8192, 2048], P('tok', 'head'), may hold values from -6 to 6
- upstream: bfloat16 [2, 8192, 2048], P(None, 'tok', 'head'), may hold values from -6 to 6
- out_gain: float32 [2048], P('head'), may hold values from 0.5 to 2
- gate_weight: bfloat16 [4, 512, 512], P('head', 'tok'), may hold values from -0.25 to 0.25
- up_weight: bfloat16 [4, 512, 512], P('head', 'tok'), may hold values from -0.25 to 0.25
- down_weight: bfloat16 [4, 512, 512], P('head', 'tok'), may hold values from -0.25 to 0.25
Outputs:
- grad_queries: bfloat16 [2, 8192, 2048], P(None, 'tok', 'head')
- grad_keys: bfloat16 [8192, 2048], P('tok', 'head')
- grad_values: bfloat16 [8192, 2048], P('tok', 'head')
- grad_gate: float32 [4, 512, 512], P('head', 'tok')
- grad_up: float32 [4, 512, 512], P('head', 'tok')
- grad_down: float32 [4, 512, 512], P('head', 'tok')
All inputs are finite; a program needn't handle non-finite values.
Results may differ from a plain program's by a relative error of at most 0.02.
Values may be sent and summed in bfloat16 or wider, within the bound.
A program may use at most 128 MiB of HBM per device.

v0:
```python
import math
import jax
import jax.numpy as jnp
from jax import lax
from jax.sharding import PartitionSpec as P

NS_STEPS = 2
lin_coef = 3.4445
cube_coef = -4.775
fifth_coef = 2.0315
rms_eps = 1e-06
fro_eps = 1e-07


def product(left, right):
    return jnp.dot(left, right, preferred_element_type=jnp.float32)


def across(left, right):
    return lax.dot_general(
        left, right, (((0,), (0,)), ((), ())), preferred_element_type=jnp.float32
    )


def against(left, right):
    return lax.dot_general(
        left, right, (((1,), (1,)), ((), ())), preferred_element_type=jnp.float32
    )


def fast_forward(keys, values, weights):
    gate_weight, up_weight, down_weight = weights
    gate_pre = product(keys, gate_weight)
    up_pre = product(keys, up_weight)
    sigma = jax.nn.sigmoid(gate_pre)
    active = gate_pre * sigma
    hidden = (active * up_pre).astype(jnp.bfloat16)
    back = -against(values, down_weight)
    slope = sigma * (1.0 + gate_pre * (1.0 - sigma))
    d_gate = (back * up_pre * slope).astype(jnp.bfloat16)
    d_up = (back * active).astype(jnp.bfloat16)
    fast = (across(keys, d_gate), across(keys, d_up), -across(hidden, values))
    saved = (gate_pre, up_pre, sigma, active, hidden, back, slope, d_gate, d_up)
    return (fast, saved)


def fast_second(keys, values, weights, saved, cots):
    gate_weight, up_weight, down_weight = weights
    gate_pre, up_pre, sigma, active, hidden, back, slope, d_gate, d_up = saved
    cot_gate, cot_up, cot_down = cots
    along_gate = product(keys, cot_gate)
    along_up = product(keys, cot_up)
    along_hidden = -against(values, cot_down)
    curve = sigma * (1.0 - sigma) * (2.0 + gate_pre * (1.0 - 2.0 * sigma))
    d_back = (along_gate * up_pre * slope + along_up * active).astype(jnp.bfloat16)
    d_upper = (along_gate * back * slope + along_hidden * active).astype(jnp.bfloat16)
    d_lower = (
        along_gate * back * up_pre * curve + along_up * back * slope + along_hidden * up_pre * slope
    ).astype(jnp.bfloat16)
    grad_keys = (
        against(d_gate, cot_gate)
        + against(d_up, cot_up)
        + against(d_lower, gate_weight)
        + against(d_upper, up_weight)
    ).astype(jnp.bfloat16)
    grad_values = (-product(hidden, cot_down) - product(d_back, down_weight)).astype(jnp.bfloat16)
    partial_value = (across(keys, d_lower), across(keys, d_upper), -across(d_back, values))
    return (grad_keys, grad_values, partial_value)


def apply_forward(queries, weights):
    gate_weight, up_weight, down_weight = weights
    gate_pre = product(queries, gate_weight)
    up_pre = product(queries, up_weight)
    sigma = jax.nn.sigmoid(gate_pre)
    hidden = (gate_pre * sigma * up_pre).astype(jnp.bfloat16)
    output = product(hidden, down_weight)
    return (gate_pre, up_pre, sigma, hidden, output)


def statistics(output, upstream, out_gain, width):
    weighted = out_gain * upstream.astype(jnp.float32)
    sums = lax.psum((jnp.sum(output * output, axis=1), jnp.sum(weighted * output, axis=1)), "head")
    return (lax.rsqrt(sums[0] / width + rms_eps), sums[1] / width)


def apply_backward(queries, weights, saved, upstream, out_gain, width):
    gate_weight, up_weight, down_weight = weights
    gate_pre, up_pre, sigma, hidden, output = saved
    inverse_rms, mean_dot = statistics(output, upstream, out_gain, width)
    weighted = out_gain * upstream.astype(jnp.float32)
    d_output = (
        inverse_rms[:, None] * weighted
        - output * (inverse_rms * inverse_rms * inverse_rms * mean_dot)[:, None]
    ).astype(jnp.bfloat16)
    back = against(d_output, down_weight)
    slope = sigma * (1.0 + gate_pre * (1.0 - sigma))
    d_gate = (back * up_pre * slope).astype(jnp.bfloat16)
    d_up = (back * gate_pre * sigma).astype(jnp.bfloat16)
    grad_queries = (against(d_gate, gate_weight) + against(d_up, up_weight)).astype(jnp.bfloat16)
    partial_value = (across(queries, d_gate), across(queries, d_up), across(hidden, d_output))
    return (grad_queries, partial_value)


def schulz_forward(begin):
    current = begin
    saved = []
    for sweep in range(NS_STEPS):
        gram = against(current, current).astype(jnp.bfloat16)
        blend = (cube_coef * gram.astype(jnp.float32) + fifth_coef * product(gram, gram)).astype(
            jnp.bfloat16
        )
        following = (lin_coef * current.astype(jnp.float32) + product(blend, current)).astype(
            jnp.bfloat16
        )
        saved.append((current, gram, blend))
        current = following
    return (current, saved)


def schulz_backward(cotan, saved):
    current = cotan
    for iterate, gram, blend in reversed(saved):
        cross = against(current, iterate)
        symmetric = (cross + cross.T).astype(jnp.bfloat16)
        bent = product(symmetric, gram)
        mixed = (cube_coef * symmetric.astype(jnp.float32) + fifth_coef * (bent + bent.T)).astype(
            jnp.bfloat16
        )
        current = (
            lin_coef * current.astype(jnp.float32)
            + product(blend, current)
            + product(mixed, iterate)
        ).astype(jnp.bfloat16)
    return current


def per_device(queries, keys, values, upstream, out_gain, gate_weight, up_weight, down_weight):
    shards = lax.axis_size("tok")
    owner = lax.axis_index("tok")
    width = out_gain.shape[0] * lax.axis_size("head")
    scale = 1.0 / math.sqrt(queries.shape[1] * shards)
    own_rows = (gate_weight[0], up_weight[0], down_weight[0])
    starts = [owner * own_rows[which].shape[0] for which in range(3)]
    first = (
        lax.all_gather(own_rows[0], "tok", axis=0, tiled=True),
        lax.all_gather(own_rows[1], "tok", axis=0, tiled=True),
        lax.all_gather(own_rows[2], "tok", axis=0, tiled=True),
    )
    fast, saved_keys = fast_forward(keys, values, first)
    apply_first = apply_forward(queries[0], first)
    grad_first, partial_first = apply_backward(
        queries[0], first, apply_first, upstream[0], out_gain, width
    )
    totals = lax.psum((fast[0], fast[1], fast[2]), "tok")
    roots = [jnp.sqrt(jnp.sum(totals[which] * totals[which])) for which in range(3)]
    forward = [
        schulz_forward((totals[which] / (roots[which] + fro_eps)).astype(jnp.bfloat16))
        for which in range(3)
    ]
    finals = [forward[which][0] for which in range(3)]
    second = tuple(
        (
            (first[which].astype(jnp.float32) - finals[which].astype(jnp.float32)).astype(
                jnp.bfloat16
            )
            for which in range(3)
        )
    )
    apply_second = apply_forward(queries[1], second)
    grad_second, partial_second = apply_backward(
        queries[1], second, apply_second, upstream[1], out_gain, width
    )
    rates = lax.psum((partial_second[0], partial_second[1], partial_second[2]), "tok")
    bottoms = [
        schulz_backward((-rates[which]).astype(jnp.bfloat16), forward[which][1])
        for which in range(3)
    ]
    cots = []
    for which in range(3):
        norm = roots[which] + fro_eps
        inner = jnp.sum(bottoms[which].astype(jnp.float32) * totals[which])
        cots.append(
            (
                bottoms[which].astype(jnp.float32) / norm
                - totals[which] * (inner / (norm * norm * roots[which]))
            ).astype(jnp.bfloat16)
        )
    rate_rows = [
        lax.dynamic_slice_in_dim(rates[which], starts[which], own_rows[which].shape[0], 0)
        for which in range(3)
    ]
    grad_keys, grad_values, second_order = fast_second(keys, values, first, saved_keys, cots)
    sums = (
        lax.psum_scatter(
            partial_first[0] + second_order[0], "tok", scatter_dimension=0, tiled=True
        ),
        lax.psum_scatter(
            partial_first[1] + second_order[1], "tok", scatter_dimension=0, tiled=True
        ),
        lax.psum_scatter(
            partial_first[2] + second_order[2], "tok", scatter_dimension=0, tiled=True
        ),
    )
    grad_gate = ((sums[0] + rate_rows[0]) * scale)[None]
    grad_up = ((sums[1] + rate_rows[1]) * scale)[None]
    grad_down = ((sums[2] + rate_rows[2]) * scale)[None]
    grad_queries = jnp.stack([grad_first, grad_second])
    return (grad_queries, grad_keys, grad_values, grad_gate, grad_up, grad_down)


def solution(mesh):
    in_specs = (
        P(None, "tok", "head"),
        P("tok", "head"),
        P("tok", "head"),
        P(None, "tok", "head"),
        P("head"),
        P("head", "tok", None),
        P("head", "tok", None),
        P("head", "tok", None),
    )
    out_specs = (
        P(None, "tok", "head"),
        P("tok", "head"),
        P("tok", "head"),
        P("head", "tok", None),
        P("head", "tok", None),
        P("head", "tok", None),
    )
    return jax.shard_map(
        per_device, mesh=mesh, in_specs=in_specs, out_specs=out_specs, check_vma=False
    )
```

profile of v0, /device:TPU:8, one launch (start us, length us, event | category | flops | bytes accessed | tf_op | source)
XLA Modules:
  0.0 1135.4 jit_solution(10835314642906359188)
XLA Ops:
  7.2 53.5 %all-gather = bf16[1,512,512]{2,1,0:T(8,128)(2,1)S(1)} all-gather(bf16[1,8,512]{2,1,0:T(8,128)(2,1)} %param.13), channel_id=2, replica_groups=mesh['tok'=64,'head'=4] {'tok'}, dimensions={1}, use_global_device_ids=true | all-gather | bytes 532480 | tf_op jit(solution)/shard_map/all_gather | solution.py:146
  60.8 49.5 %all-gather.2 = bf16[1,512,512]{2,1,0:T(8,128)(2,1)S(1)} all-gather(bf16[1,8,512]{2,1,0:T(8,128)(2,1)S(1)} %copy-done.104), channel_id=4, replica_groups=mesh['tok'=64,'head'=4] {'tok'}, dimensions={1}, use_global_device_ids=true | all-gather | bytes 532480 | tf_op jit(solution)/shard_map/all_gather | solution.py:148
  110.2 48.1 %all-gather.1 = bf16[1,512,512]{2,1,0:T(8,128)(2,1)S(1)} all-gather(bf16[1,8,512]{2,1,0:T(8,128)(2,1)S(1)} %copy-done.105), channel_id=3, replica_groups=mesh['tok'=64,'head'=4] {'tok'}, dimensions={1}, use_global_device_ids=true | all-gather | bytes 532480 | tf_op jit(solution)/shard_map/all_gather | solution.py:147
  169.9 186.9 %all-reduce.8.cloned.1.call-done = (f32[512,512]{0,1:T(8,128)}, f32[512,512]{0,1:T(8,128)}, f32[512,512]{0,1:T(8,128)}) async-done(((f32[512,512]{0,1:T(8,128)}, f32[512,512]{0,1:T(8,128)}, f32[512,512]{0,1:T(8,128)}), (f32[512,512]{0,1:T(8,128)}, f32[512,512]{0,1:T(8,128)}, f32[512,512]{0,1:T(8,128)})) %all-reduce.8.cloned.1.call-update) | async-done | bytes 3145744 | tf_op jit(solution)/shard_map/psum | solution.py:155
  356.8 2.2 multiply_reduce_fusion.2
  386.3 9.2 all-reduce.2
  402.8 2.1 multiply_convert_fusion.6
  406.8 188.1 %all-reduce.6.cloned.1.call-done = (f32[512,512]{0,1:T(8,128)}, f32[512,512]{0,1:T(8,128)}, f32[512,512]{0,1:T(8,128)}) async-done(((f32[512,512]{0,1:T(8,128)}, f32[512,512]{0,1:T(8,128)}, f32[512,512]{0,1:T(8,128)}), (f32[512,512]{0,1:T(8,128)}, f32[512,512]{0,1:T(8,128)}, f32[512,512]{0,1:T(8,128)})) %all-reduce.6.cloned.1.call-update) | async-done | bytes 3145744 | tf_op jit(solution)/shard_map/psum | solution.py:174
  594.9 3.3 convolution_add_fusion.13
  599.7 2.6 copy.72
  606.2 2.6 copy.73
  608.8 2.7 fusion.30
  617.4 2.6 copy.80
  624.0 2.6 copy.81
  626.5 2.7 fusion.32
  635.1 2.6 copy.91
  641.7 2.6 copy.92
  644.2 2.7 fusion.34
  650.0 2.5 copy.76
  656.5 2.5 copy.77
  659.1 2.6 copy.84
  665.6 2.6 copy.85
  668.2 4.1 fusion.45
  672.9 4.4 fusion.48
  678.0 2.9 fusion.44
  682.8 2.6 copy.95
  689.3 3.8 fusion.51
  699.4 2.5 copy.128
  704.4 2.5 copy.130
  720.7 120.6 %reduce-scatter.10.cloned.1.call-done = f32[8,512]{1,0:T(8,128)} async-done(((f32[512,512]{1,0:T(8,128)}), f32[8,512]{1,0:T(8,128)}) %reduce-scatter.10.cloned.1.call-update) | async-done | bytes 16400
  843.9 139.7 %reduce-scatter.12.cloned.1.call-done = f32[8,512]{1,0:T(8,128)} async-done(((f32[512,512]{1,0:T(8,128)}), f32[8,512]{1,0:T(8,128)}) %reduce-scatter.12.cloned.1.call-update) | async-done | bytes 16400
  986.3 139.7 %reduce-scatter.14.cloned.1.call-done = f32[8,512]{1,0:T(8,128)} async-done(((f32[512,512]{1,0:T(8,128)}), f32[8,512]{1,0:T(8,128)}) %reduce-scatter.14.cloned.1.call-update) | async-done | bytes 16400
  (329 shorter events, 116.8 us)
Async XLA Ops:
  7.2 151.2 %copy-start = (bf16[128,512]{1,0:T(8,128)(2,1)S(1)}, bf16[128,512]{1,0:T(8,128)(2,1)}, u32[]{:S(2)}) copy-start(bf16[128,512]{1,0:T(8,128)(2,1)} %param.9) | copy-start | bytes 393220
  7.2 53.6 %copy-start.104 = (bf16[1,8,512]{2,1,0:T(8,128)(2,1)S(1)}, bf16[1,8,512]{2,1,0:T(8,128)(2,1)}, u32[]{:S(2)}) copy-start(bf16[1,8,512]{2,1,0:T(8,128)(2,1)} %param.15) | copy-start | bytes 24580
  7.2 349.6 %all-reduce.8.cloned.1.call-start = ((), (), s32[]{:S(2)}) async-start(), calls=%async_computation.7 | async-start | bytes 6291456 | tf_op jit(solution)/shard_map/psum | solution.py:155
  60.8 49.5 %copy-start.105 = (bf16[1,8,512]{2,1,0:T(8,128)(2,1)S(1)}, bf16[1,8,512]{2,1,0:T(8,128)(2,1)}, u32[]{:S(2)}) copy-start(bf16[1,8,512]{2,1,0:T(8,128)(2,1)} %param.14) | copy-start | bytes 24580
  158.4 10.5 copy-start.5
  161.0 2.7 copy-start.48
  165.1 429.9 %all-reduce.6.cloned.1.call-start = ((), (), s32[]{:S(2)}) async-start(), calls=%async_computation.6 | async-start | bytes 6291456 | tf_op jit(solution)/shard_map/psum | solution.py:174
  356.8 2.9 copy-start.2
  364.2 2.6 copy-start.3
  375.5 1.8 copy-start.16
  378.1 4.8 copy-start.26
  380.8 2.1 copy-start.41
  383.7 2.6 copy-start.60
  384.2 2.1 copy-start.40
  396.2 2.0 copy-start.59
  402.5 438.7 %reduce-scatter.10.cloned.1.call-start = ((), (), s32[]{:S(2)}) async-start(), calls=%async_computation.3 | async-start | bytes 1064960
  594.9 3.3 copy-start.9
  594.9 3.3 copy-start.32
  602.3 2.6 copy-start.84
  608.8 2.7 copy-start.80
  620.0 2.6 copy-start.82
  626.5 2.7 copy-start.76
  637.7 2.6 copy-start.78
  644.2 2.7 copy-start.74
  652.5 2.6 copy-start.70
  661.6 2.5 copy-start.72
  682.8 2.6 copy-start.4
  685.4 2.2 copy-start.68
  696.3 1.8 copy-start.24
  697.4 5.7 copy-start.91
  701.9 281.7 %reduce-scatter.12.cloned.1.call-start = ((), (), s32[]{:S(2)}) async-start(), calls=%async_computation.4 | async-start | bytes 1064960
  707.0 419.0 %reduce-scatter.14.cloned.1.call-start = ((), (), s32[]{:S(2)}) async-start(), calls=%async_computation.5 | async-start | bytes 1064960
  (83 other events, 90.3 us)
Sparse Core Ops, SparseCore 0:
  165.2 191.5 all-reduce.7
  402.7 192.2 all-reduce.5
  702.1 139.1 reduce-scatter.9
  845.1 138.5 reduce-scatter.11
  987.5 138.5 reduce-scatter.13
where the time goes:
time: 1140 us
  waiting for transfers between devices  775 us (68%)
  blocking collectives  160 us (14%)
  matrix products  85.5 us (8%)
  local copies, waits for them, and re-layouts  69.9 us (6%)
  other arithmetic  24.7 us (2%)
  between operations  19 us (2%)
    unnamed x8, waiting for transfers between devices  400 us
    psum x1, waiting for transfers between devices, per_device(): lax.psum((partial_second[0], partial_second[1], partial_second[2]), 'tok')  188 us
    psum x1, waiting for transfers between devices, per_device(): totals = lax.psum((fast[0], fast[1], fast[2]), 'tok')  187 us
    dot_general x42, matrix products, product(): return jnp.dot(left, right, preferred_element_type=jnp.float32)  54.5 us
    all_gather x1, blocking collectives, per_device(): lax.all_gather(own_rows[0], 'tok', axis=0, tiled=True)  53.5 us
    all_gather x1, blocking collectives, per_device(): lax.all_gather(own_rows[2], 'tok', axis=0, tiled=True)  49.5 us
    all_gather x1, blocking collectives, per_device(): lax.all_gather(own_rows[1], 'tok', axis=0, tiled=True)  48.1 us
    unnamed x228, local copies, waits for them, and re-layouts  37.3 us
  transfers between devices with their start and end apart: 5, of which 5 were waited for; matrix products, arithmetic and copies ran while one was open for 2% of the time, Pallas kernels for 0%

commit v1 on v0

--- a/solution.py
+++ b/solution.py
@@ -10,6 +10,13 @@
 fifth_coef = 2.0315
 rms_eps = 1e-06
 fro_eps = 1e-07
+
+
+def exchange_gather(block, axis, dim):
+    size = lax.axis_size(axis)
+    blocks = jnp.stack([block for _ in range(size)])
+    blocks = lax.all_to_all(blocks, axis, split_axis=0, concat_axis=0)
+    return jnp.concatenate(blocks, axis=dim)
 
 
 def product(left, right):
@@ -143,7 +150,7 @@
     own_rows = (gate_weight[0], up_weight[0], down_weight[0])
     starts = [owner * own_rows[which].shape[0] for which in range(3)]
     first = (
-        lax.all_gather(own_rows[0], "tok", axis=0, tiled=True),
+        exchange_gather(own_rows[0], "tok", 0),
         lax.all_gather(own_rows[1], "tok", axis=0, tiled=True),
         lax.all_gather(own_rows[2], "tok", axis=0, tiled=True),
     )

time: 1140 us -> 1110 us (0.974)
  blocking collectives: 160 us -> 116 us
  starting transfers between devices: 0.84 us -> 12.7 us
    all_gather x1 -> x0, blocking collectives: 53.5 us -> none  [per_device(): lax.all_gather(own_rows[0], 'tok', axis=0, tiled=True)]
    all_to_all x0 -> x1, starting transfers between devices: none -> 12.1 us  [exchange_gather(): blocks = lax.all_to_all(blocks, axis, split_axis=0, concat_axis=0)]
  transfers between devices with their start and end apart: 5 -> 6, of which waited for: 5 -> 5; matrix products, arithmetic and copies ran while one was open for 2% -> 2% of each run, Pallas kernels for 0% -> 0%
where the time goes in v1:
time: 1110 us; the launch traced here: 1100 us
  waiting for transfers between devices  776 us (70%)
  blocking collectives  116 us (10%)
  matrix products  85.4 us (8%)
  local copies, waits for them, and re-layouts  70.8 us (6%)
  other arithmetic  24.7 us (2%)
  between operations  18.8 us (2%)
  starting transfers between devices  12.7 us (1%)
    unnamed x8, waiting for transfers between devices  400 us
    psum x1, waiting for transfers between devices, per_device(): lax.psum((partial_second[0], partial_second[1], partial_second[2]), 'tok')  188 us
    psum x1, waiting for transfers between devices, per_device(): totals = lax.psum((fast[0], fast[1], fast[2]), 'tok')  187 us
    all_gather x1, blocking collectives, per_device(): lax.all_gather(own_rows[2], 'tok', axis=0, tiled=True)  57.5 us
    dot_general x42, matrix products, product(): return jnp.dot(left, right, preferred_element_type=jnp.float32)  54.5 us
    all_gather x1, blocking collectives, per_device(): lax.all_gather(own_rows[1], 'tok', axis=0, tiled=True)  49.6 us
    unnamed x228, local copies, waits for them, and re-layouts  36.6 us
  transfers between devices with their start and end apart: 6, of which 5 were waited for; matrix products, arithmetic and copies ran while one was open for 2% of the time, Pallas kernels for 0%

profile of v1, /device:TPU:8, one launch (start us, length us, event | category | flops | bytes accessed | tf_op | source)
XLA Modules:
  0.0 1104.6 jit_solution(12973535871493212892)
XLA Ops:
  8.7 12.1 %all-to-all-start = ((bf16[64,8,512]{2,1,0:T(8,128)(2,1)}), bf16[64,8,512]{2,1,0:T(8,128)(2,1)S(1)}, u32[]{:S(2)}, u32[]{:S(2)}) async-start(bf16[64,8,512]{2,1,0:T(8,128)(2,1)} %stack.12), calls=%async_computation | async-start | bytes 1048576 | tf_op jit(solution)/shard_map/all_to_all | solution.py:18
  20.9 57.5 %all-gather.1 = bf16[1,512,512]{2,1,0:T(8,128)(2,1)S(1)} all-gather(bf16[1,8,512]{2,1,0:T(8,128)(2,1)S(1)} %copy-done.104), channel_id=3, replica_groups=mesh['tok'=64,'head'=4] {'tok'}, dimensions={1}, use_global_device_ids=true | all-gather | bytes 532480 | tf_op jit(solution)/shard_map/all_gather | solution.py:155
  78.4 49.6 %all-gather = bf16[1,512,512]{2,1,0:T(8,128)(2,1)S(1)} all-gather(bf16[1,8,512]{2,1,0:T(8,128)(2,1)S(1)} %copy-done.105), channel_id=2, replica_groups=mesh['tok'=64,'head'=4] {'tok'}, dimensions={1}, use_global_device_ids=true | all-gather | bytes 532480 | tf_op jit(solution)/shard_map/all_gather | solution.py:154
  138.5 187.4 %all-reduce.8.cloned.1.call-done = (f32[512,512]{0,1:T(8,128)}, f32[512,512]{0,1:T(8,128)}, f32[512,512]{0,1:T(8,128)}) async-done(((f32[512,512]{0,1:T(8,128)}, f32[512,512]{0,1:T(8,128)}, f32[512,512]{0,1:T(8,128)}), (f32[512,512]{0,1:T(8,128)}, f32[512,512]{0,1:T(8,128)}, f32[512,512]{0,1:T(8,128)})) %all-reduce.8.cloned.1.call-update) | async-done | bytes 3145744 | tf_op jit(solution)/shard_map/psum | solution.py:162
  325.9 2.2 multiply_reduce_fusion.2
  355.5 9.2 all-reduce.2
  372.0 2.1 multiply_convert_fusion.6
  376.0 188.4 %all-reduce.6.cloned.1.call-done = (f32[512,512]{0,1:T(8,128)}, f32[512,512]{0,1:T(8,128)}, f32[512,512]{0,1:T(8,128)}) async-done(((f32[512,512]{0,1:T(8,128)}, f32[512,512]{0,1:T(8,128)}, f32[512,512]{0,1:T(8,128)}), (f32[512,512]{0,1:T(8,128)}, f32[512,512]{0,1:T(8,128)}, f32[512,512]{0,1:T(8,128)})) %all-reduce.6.cloned.1.call-update) | async-done | bytes 3145744 | tf_op jit(solution)/shard_map/psum | solution.py:181
  564.4 3.3 convolution_add_fusion.13
  569.1 2.6 copy.117
  575.6 2.6 copy.118
  578.2 2.7 fusion.30
  586.8 2.6 copy.125
  593.4 2.6 copy.126
  595.9 2.7 fusion.32
  604.5 2.6 copy.136
  611.1 2.6 copy.137
  613.6 2.7 fusion.34
  619.4 2.5 copy.121
  625.9 2.5 copy.122
  628.4 2.6 copy.129
  635.0 2.6 copy.130
  637.5 4.1 fusion.45
  642.3 4.4 fusion.48
  647.4 3.0 fusion.44
  652.2 2.6 copy.140
  658.8 3.8 fusion.51
  668.8 2.5 copy.173
  673.8 2.5 copy.175
  690.1 120.6 %reduce-scatter.10.cloned.1.call-done = f32[8,512]{1,0:T(8,128)} async-done(((f32[512,512]{1,0:T(8,128)}), f32[8,512]{1,0:T(8,128)}) %reduce-scatter.10.cloned.1.call-update) | async-done | bytes 16400
  813.3 139.8 %reduce-scatter.12.cloned.1.call-done = f32[8,512]{1,0:T(8,128)} async-done(((f32[512,512]{1,0:T(8,128)}), f32[8,512]{1,0:T(8,128)}) %reduce-scatter.12.cloned.1.call-update) | async-done | bytes 16400
  955.7 139.7 %reduce-scatter.14.cloned.1.call-done = f32[8,512]{1,0:T(8,128)} async-done(((f32[512,512]{1,0:T(8,128)}), f32[8,512]{1,0:T(8,128)}) %reduce-scatter.14.cloned.1.call-update) | async-done | bytes 16400
  (331 shorter events, 117.3 us)
Async XLA Ops:
  7.2 121.2 %copy-start = (bf16[128,512]{1,0:T(8,128)(2,1)S(1)}, bf16[128,512]{1,0:T(8,128)(2,1)}, u32[]{:S(2)}) copy-start(bf16[128,512]{1,0:T(8,128)(2,1)} %param.9) | copy-start | bytes 393220
  8.7 12.1 %copy-start.104 = (bf16[1,8,512]{2,1,0:T(8,128)(2,1)S(1)}, bf16[1,8,512]{2,1,0:T(8,128)(2,1)}, u32[]{:S(2)}) copy-start(bf16[1,8,512]{2,1,0:T(8,128)(2,1)} %param.15) | copy-start | bytes 24580
  8.7 119.6 %all-to-all-start = ((bf16[64,8,512]{2,1,0:T(8,128)(2,1)}), bf16[64,8,512]{2,1,0:T(8,128)(2,1)S(1)}, u32[]{:S(2)}, u32[]{:S(2)}) async-start(bf16[64,8,512]{2,1,0:T(8,128)(2,1)} %stack.12), calls=%async_computation | async-start | bytes 1048576 | tf_op jit(solution)/shard_map/all_to_all | solution.py:18
  20.8 57.6 %copy-start.105 = (bf16[1,8,512]{2,1,0:T(8,128)(2,1)S(1)}, bf16[1,8,512]{2,1,0:T(8,128)(2,1)}, u32[]{:S(2)}) copy-start(bf16[1,8,512]{2,1,0:T(8,128)(2,1)} %param.14) | copy-start | bytes 24580
  20.8 305.1 %all-reduce.8.cloned.1.call-start = ((), (), s32[]{:S(2)}) async-start(), calls=%async_computation.8 | async-start | bytes 6291456 | tf_op jit(solution)/shard_map/psum | solution.py:162
  78.4 49.6 %copy-start.33 = (bf16[128,512]{1,0:T(8,128)(2,1)S(1)}, bf16[128,512]{1,0:T(8,128)(2,1)}, u32[]{:S(2)}) copy-start(bf16[128,512]{1,0:T(8,128)(2,1)} %param.10) | copy-start | bytes 393220
  128.0 9.5 copy-start.5
  130.0 2.7 copy-start.48
  134.0 430.4 %all-reduce.6.cloned.1.call-start = ((), (), s32[]{:S(2)}) async-start(), calls=%async_computation.7 | async-start | bytes 6291456 | tf_op jit(solution)/shard_map/psum | solution.py:181
  325.9 2.9 copy-start.2
  333.4 2.6 copy-start.3
  347.3 4.8 copy-start.26
  350.0 2.1 copy-start.41
  352.9 2.7 copy-start.60
  353.3 2.2 copy-start.40
  365.4 2.0 copy-start.59
  371.7 439.0 %reduce-scatter.10.cloned.1.call-start = ((), (), s32[]{:S(2)}) async-start(), calls=%async_computation.4 | async-start | bytes 1064960
  564.4 3.3 copy-start.9
  564.4 3.3 copy-start.32
  571.7 2.6 copy-start.84
  578.2 2.7 copy-start.80
  589.4 2.6 copy-start.82
  595.9 2.7 copy-start.76
  607.1 2.6 copy-start.78
  613.6 2.7 copy-start.74
  621.9 2.6 copy-start.70
  631.0 2.6 copy-start.72
  652.2 2.6 copy-start.4
  654.8 2.2 copy-start.68
  666.8 5.7 copy-start.91
  671.4 281.7 %reduce-scatter.12.cloned.1.call-start = ((), (), s32[]{:S(2)}) async-start(), calls=%async_computation.5 | async-start | bytes 1064960
  676.4 419.0 %reduce-scatter.14.cloned.1.call-start = ((), (), s32[]{:S(2)}) async-start(), calls=%async_computation.6 | async-start | bytes 1064960
  (84 other events, 92.9 us)
Sparse Core Ops, SparseCore 0:
  134.1 191.7 all-reduce.7
  371.8 192.5 all-reduce.5
  671.5 139.1 reduce-scatter.9
  814.5 138.5 reduce-scatter.11
  956.9 138.4 reduce-scatter.13
